TPU v7x, 256 devices: a whole 4x4x8 slice. The times are simulated.
256 devices in a mesh: bank: 128 (over y, z, x), sub: 2 (over core).
Axes of the slice: x: 4, y: 4, z: 8, core: 2. Of those that a mesh axis runs over, the one named last changes fastest.
Arguments:
- embeddings: bfloat16 [786432, 1024], P(('bank', 'sub'))
- pivots: int32 [2, 256], replicated, may hold values from 0 to 786431, as said below
Outputs:
- basis: float32 [786432, 512], P(('bank', 'sub'))
- triangle: float32 [512, 512], replicated
Inputs may be any that keep to these rules, and one draw needn't show every extreme that they name: All 512 entries are distinct molecules. Molecule g lies on device g // 3072 of bank+sub (bank slowest). Each device holds at most 1 pivots of each block step, and some device holds exactly 1.
All inputs are finite; a program needn't handle non-finite values.
Results may differ from a plain program's by a relative error of at most 0.0003.
Values may be sent and summed in bfloat16 or wider, within the bound.
A program may use at most 64 MiB of HBM per device.

v0:
```python
import jax
import jax.numpy as jnp
from jax import lax
from jax.sharding import PartitionSpec as P

P_SIZE = 256


def lower_inverse(factor):
    identity = jnp.eye(factor.shape[0], dtype=factor.dtype)
    return lax.linalg.triangular_solve(factor, identity, left_side=True, lower=True)


def times_transposed(left, right, exact):
    if exact:
        return lax.dot_general(
            left,
            right,
            (((1,), (1,)), ((), ())),
            precision=lax.Precision.HIGHEST,
            preferred_element_type=jnp.float32,
        )
    return lax.dot_general(
        left, right, (((1,), (1,)), ((), ())), preferred_element_type=jnp.float32
    )


def per_device(embeddings, pivots):
    device_count = lax.axis_size(("bank", "sub"))
    my_index = lax.axis_index(("bank", "sub"))
    row_count = embeddings.shape[0]
    start_row = my_index * row_count
    flat_list = pivots.reshape(-1)
    present = (flat_list >= start_row) & (flat_list < start_row + row_count)
    local_index = jnp.clip(flat_list - start_row, 0, row_count - 1)
    picked = jnp.take(embeddings, local_index, axis=0).astype(jnp.float32) * present[
        :, None
    ].astype(jnp.float32)
    chosen = lax.psum(picked, ("bank", "sub")).astype(jnp.bfloat16)
    norms = jnp.einsum("rd,rd->r", embeddings, embeddings, preferred_element_type=jnp.float32)
    chosen_norms = jnp.einsum("rd,rd->r", chosen, chosen, preferred_element_type=jnp.float32)
    dots = times_transposed(embeddings, chosen, False)
    similar = dots / (norms[:, None] + chosen_norms[None, :] - dots)
    block_dots = times_transposed(chosen, chosen, False)
    block = block_dots / (chosen_norms[:, None] + chosen_norms[None, :] - block_dots)
    first_inverse = lower_inverse(jnp.linalg.cholesky(block[:P_SIZE, :P_SIZE]))
    first_factor = times_transposed(similar[:, :P_SIZE], first_inverse, True)
    pivot_first = times_transposed(block[P_SIZE:, :P_SIZE], first_inverse, True)
    second_cols = similar[:, P_SIZE:] - times_transposed(first_factor, pivot_first, True)
    second_block = block[P_SIZE:, P_SIZE:] - times_transposed(pivot_first, pivot_first, True)
    second_inverse = lower_inverse(jnp.linalg.cholesky(second_block))
    second_factor = times_transposed(second_cols, second_inverse, True)
    factor = jnp.concatenate([first_factor, second_factor], axis=1)
    total_rows = row_count * device_count
    local_gram = (
        lax.dot_general(
            factor,
            factor,
            (((0,), (0,)), ((), ())),
            precision=lax.Precision.HIGHEST,
            preferred_element_type=jnp.float32,
        )
        / total_rows
    )
    gram = lax.psum(local_gram, ("bank", "sub"))
    lower_root = jnp.linalg.cholesky(gram)
    basis = times_transposed(factor, lower_inverse(lower_root), True)
    return (basis, lower_root.T)


def solution(mesh):
    in_specs = (P(("bank", "sub"), None), P())
    out_specs = (P(("bank", "sub"), None), P())
    return jax.shard_map(
        per_device, mesh=mesh, in_specs=in_specs, out_specs=out_specs, check_vma=False
    )
```

profile of v0, /device:TPU:2, one launch (start us, length us, event | category | flops | bytes accessed | tf_op | source)
XLA Modules:
  0.0 711.0 jit_solution(15264910173335622265)
XLA Ops:
  8.7 4.1 fusion
  12.8 6.3 gather_fusion
  19.5 87.7 %all-reduce.6 = bf16[512,1024]{1,0:T(8,128)(2,1)S(1)} all-reduce(f32[512,1024]{1,0:T(8,128)S(1)} %convert_multiply_fusion.2), channel_id=1, replica_groups=mesh['bank'=128,'sub'=2] {'bank','sub'}, use_global_device_ids=true, to_apply=%region_0.1 | all-reduce | flops 524288 | bytes 3145728 | tf_op jit(solution)/shard_map/psum | solution.py:39
  108.4 11.7 %cholesky.357 = f32[128,128]{1,0:T(8,128)S(1)} custom-call(f32[128,128]{1,0:T(8,128)S(1)} %cholesky.407), custom_call_target="Cholesky" | custom-call | tf_op jit(solution)/shard_map/jit(cholesky)/cholesky | solution.py:46
  120.2 9.8 %custom-call.43 = f32[1,128,128]{1,2,0:T(8,128)S(1)} custom-call(f32[1,128,128]{2,1,0:T(8,128)S(1)} %get-tuple-element.80), custom_call_target="InvertDiagBlocksLowerTriangular" | custom-call | tf_op jit(solution)/shard_map/jit(cholesky)/cholesky/custom-call.1 | solution.py:46
  130.5 11.7 %cholesky.367 = f32[128,128]{1,0:T(8,128)S(1)} custom-call(f32[128,128]{1,0:T(8,128)S(1)} %convolution_subtract_fusion.10), custom_call_target="Cholesky" | custom-call | tf_op jit(solution)/shard_map/jit(cholesky)/cholesky | solution.py:46
  144.2 3.8 while.6
  144.8 1.3 bitcast_dynamic-update-slice_fusion.7
  146.7 1.3 bitcast_dynamic-update-slice_fusion.7
  148.0 20.1 %custom-call.44 = f32[2,128,128]{1,2,0:T(8,128)S(1)} custom-call(f32[2,128,128]{2,1,0:T(8,128)S(1)} %get-tuple-element.27), custom_call_target="InvertDiagBlocksLowerTriangular" | custom-call | tf_op jit(solution)/shard_map/triangular_solve/custom-call.9 | solution.py:11
  170.9 11.7 %cholesky.384 = f32[128,128]{1,0:T(8,128)S(1)} custom-call(f32[128,128]{1,0:T(8,128)S(1)} %cholesky.410), custom_call_target="Cholesky" | custom-call | tf_op jit(solution)/shard_map/jit(cholesky)/cholesky | solution.py:51
  182.7 9.8 %custom-call.45 = f32[1,128,128]{1,2,0:T(8,128)S(1)} custom-call(f32[1,128,128]{2,1,0:T(8,128)S(1)} %get-tuple-element.76), custom_call_target="InvertDiagBlocksLowerTriangular" | custom-call | tf_op jit(solution)/shard_map/jit(cholesky)/cholesky/custom-call.1 | solution.py:51
  193.0 11.7 %cholesky.394 = f32[128,128]{1,0:T(8,128)S(1)} custom-call(f32[128,128]{1,0:T(8,128)S(1)} %convolution_subtract_fusion.9), custom_call_target="Cholesky" | custom-call | tf_op jit(solution)/shard_map/jit(cholesky)/cholesky | solution.py:51
  207.3 3.8 while.7
  207.9 1.3 bitcast_dynamic-update-slice_fusion.8
  209.8 1.3 bitcast_dynamic-update-slice_fusion.8
  211.1 19.9 %custom-call.46 = f32[2,128,128]{1,2,0:T(8,128)S(1)} custom-call(f32[2,128,128]{2,1,0:T(8,128)S(1)} %get-tuple-element.28), custom_call_target="InvertDiagBlocksLowerTriangular" | custom-call | tf_op jit(solution)/shard_map/triangular_solve/custom-call.9 | solution.py:11
  231.9 5.7 subtract_divide_fusion
  237.6 3.0 fusion.3
  240.6 3.2 convolution_subtract_fusion
  243.8 3.0 fusion.30
  246.9 1.7 copy-done
  248.5 11.9 %fusion.17 = f32[512,512]{0,1:T(8,128)} fusion(f32[3072,256]{0,1:T(8,128)S(1)} %fusion.30, f32[3072,256]{0,1:T(8,128)S(1)} %fusion.3), kind=kOutput, calls=%fused_computation.50 | convolution fusion | flops 9665511424 | bytes 7340032 | tf_op jit(solution)/shard_map/dot_general | solution.py:56
  262.4 255.3 %all-reduce.5.cloned.1.call-done = f32[512,512]{0,1:T(8,128)} async-done(((f32[512,512]{0,1:T(8,128)}), f32[512,512]{0,1:T(8,128)}) %all-reduce.5.cloned.1.call-update) | async-done | bytes 1048592 | tf_op jit(solution)/shard_map/psum | solution.py:65
  517.8 2.5 copy.12
  520.3 1.8 fusion.14
  523.1 11.7 %cholesky.167 = f32[128,128]{1,0:T(8,128)S(1)} custom-call(f32[128,128]{1,0:T(8,128)S(1)} %cholesky.413), custom_call_target="Cholesky" | custom-call | tf_op jit(solution)/shard_map/jit(cholesky)/cholesky | solution.py:66
  536.0 9.8 %custom-call.35 = f32[1,128,128]{1,2,0:T(8,128)S(1)} custom-call(f32[1,128,128]{2,1,0:T(8,128)S(1)} %get-tuple-element.72), custom_call_target="InvertDiagBlocksLowerTriangular" | custom-call | tf_op jit(solution)/shard_map/jit(cholesky)/cholesky | solution.py:66
  545.8 1.9 constant_dynamic-update-slice_fusion.5
  549.0 11.7 %cholesky.190 = f32[128,128]{1,0:T(8,128)S(1)} custom-call(f32[128,128]{1,0:T(8,128)S(1)} %cholesky.417), custom_call_target="Cholesky" | custom-call | tf_op jit(solution)/shard_map/jit(cholesky)/cholesky | solution.py:66
  562.7 9.9 %custom-call.36 = f32[1,128,128]{1,2,0:T(8,128)S(1)} custom-call(f32[1,128,128]{2,1,0:T(8,128)S(1)} %get-tuple-element.69), custom_call_target="InvertDiagBlocksLowerTriangular" | custom-call | tf_op jit(solution)/shard_map/jit(cholesky)/cholesky | solution.py:66
  573.5 1.5 convolution_subtract_fusion.6
  575.0 11.7 %cholesky.294 = f32[128,128]{1,0:T(8,128)S(1)} custom-call(f32[128,128]{1,0:T(8,128)S(1)} %cholesky.422), custom_call_target="Cholesky" | custom-call | tf_op jit(solution)/shard_map/jit(cholesky)/cholesky | solution.py:66
  588.1 9.8 %custom-call.47 = f32[1,128,128]{1,2,0:T(8,128)S(1)} custom-call(f32[1,128,128]{2,1,0:T(8,128)S(1)} %get-tuple-element.66), custom_call_target="InvertDiagBlocksLowerTriangular" | custom-call | tf_op jit(solution)/shard_map/jit(cholesky)/cholesky/custom-call.1 | solution.py:66
  598.7 1.4 convolution_subtract_fusion.11
  600.1 11.9 %cholesky.307 = f32[128,128]{1,0:T(8,128)S(1)} custom-call(f32[128,128]{1,0:T(8,128)S(1)} %convolution_subtract_fusion.11), custom_call_target="Cholesky" | custom-call | tf_op jit(solution)/shard_map/jit(cholesky)/cholesky | solution.py:66
  615.9 2.8 fusion.16
  618.8 13.8 %while.5 = (s32[]{:T(128)}, f32[512,512]{1,0:T(8,128)}, s32[4,2]{0,1:T(2,128)S(1)}, f32[4,128,128]{2,1,0:T(8,128)}, s32[]{:T(128)}) while((s32[]{:T(128)}, f32[512,512]{1,0:T(8,128)}, s32[4,2]{0,1:T(2,128)S(1)}, f32[4,128,128]{2,1,0:T(8,128)}, s32[]{:T(128)}) %tuple.78), condition=%wide.while_cond.1, body=%wide.while_body.1.sunk | while | flops 2 | bytes 132705 | solution.py:11
  619.4 2.8 bitcast_dynamic-update-slice_fusion.6
  622.9 2.8 bitcast_dynamic-update-slice_fusion.6
  626.4 2.8 bitcast_dynamic-update-slice_fusion.6
  629.8 2.7 bitcast_dynamic-update-slice_fusion.6
  632.6 40.1 %custom-call.37 = f32[4,128,128]{1,2,0:T(8,128)S(1)} custom-call(f32[4,128,128]{2,1,0:T(8,128)} %get-tuple-element.20), custom_call_target="InvertDiagBlocksLowerTriangular" | custom-call | tf_op jit(solution)/shard_map/triangular_solve | solution.py:11
  674.0 1.4 convolution_subtract_fusion.2
  675.8 1.4 convolution_subtract_fusion.1
  677.7 1.7 convolution_subtract_fusion.4
  679.8 21.6 %fusion.1 = f32[3072,512]{1,0:T(8,128)} fusion(f32[3072,256]{0,1:T(8,128)S(1)} %copy-done.1, f32[3072,256]{0,1:T(8,128)S(1)} %fusion.3, f32[128,512]{1,0:T(8,128)S(1)} %fusion.50, f32[128,512]{1,0:T(8,128)S(1)} %fusion.51, f32[128,512]{1,0:T(8,128)S(1)} %fusion.53, f32[128,512]{1,0:T(8,128)S(1)} %fusion.37), kind=kOutput, calls=%fused_computation.11 | convolution fusion | flops 9666035712 | bytes 13631488 | tf_op jit(solution)/shard_map/dot_general | solution.py:16
  701.4 2.5 copy.14
  (101 shorter events, 29.2 us)
Async XLA Ops:
  7.2 510.6 %all-reduce.5.cloned.1.call-start = ((), (), s32[]{:S(2)}) async-start(), calls=%async_computation | async-start | bytes 2097152 | tf_op jit(solution)/shard_map/psum | solution.py:65
  7.2 161.2 %copy-start.3 = (f32[256,256]{1,0:T(8,128)}, f32[256,256]{1,0:T(8,128)S(1)}, u32[]{:S(2)}) copy-start(f32[256,256]{1,0:T(8,128)S(1)} %fusion.36) | copy-start | bytes 786436
  168.7 62.2 %copy-start.4 = (f32[256,256]{1,0:T(8,128)S(1)}, f32[256,256]{1,0:T(8,128)}, u32[]{:S(2)}) copy-start(f32[256,256]{1,0:T(8,128)} %copy-done.3) | copy-start | bytes 786436
  169.0 0.7 copy-start.5
  231.9 5.8 copy-start.6
  246.9 1.7 copy-start
  522.1 1.0 copy-start.2
  672.7 7.1 copy-start.1
Sparse Core Ops, SparseCore 0:
  260.6 257.1 all-reduce.4
where the time goes:
time: 716 us; the launch traced here: 711 us
  waiting for transfers between devices  255 us (36%)
  other arithmetic  243 us (34%)
  blocking collectives  87.7 us (12%)
  matrix products  67.7 us (9%)
  local copies, waits for them, and re-layouts  37.6 us (5%)
  between operations  19.8 us (3%)
    psum x1, waiting for transfers between devices, per_device(): gram = lax.psum(local_gram, ('bank', 'sub'))  255 us
    psum x1, blocking collectives, per_device(): chosen = lax.psum(picked, ('bank', 'sub')).astype(jnp.bfloat16)  87.7 us
    another operation x15, other arithmetic, per_device(): lower_root = jnp.linalg.cholesky(gram)  81.3 us
    another operation x7, other arithmetic, lower_inverse(): lax.linalg.triangular_solve(factor, identity, left_side=True, lower=True)  80.1 us
    another operation x7, other arithmetic, per_device(): second_inverse = lower_inverse(jnp.linalg.cholesky(second_block))  34.6 us
    another operation x6, other arithmetic, per_device(): first_inverse = lower_inverse(jnp.linalg.cholesky(block[:P_SIZE, :P_SIZE]))  34 us
    dot_general x6, matrix products, times_transposed(): lax.dot_general(left, right, (((1,), (1,)), ((), ())), precision=lax.Prec...  31.8 us
  transfers between devices with their start and end apart: 1, of which 1 were waited for; matrix products, arithmetic and copies ran while one was open for 0% of the time, Pallas kernels for 0%

commit v1 on v0

--- a/solution.py
+++ b/solution.py
@@ -36,7 +36,9 @@
     picked = jnp.take(embeddings, local_index, axis=0).astype(jnp.float32) * present[
         :, None
     ].astype(jnp.float32)
-    chosen = lax.psum(picked, ("bank", "sub")).astype(jnp.bfloat16)
+    chosen = jax.lax.psum(jax.lax.psum(picked, axis_name="sub"), axis_name="bank").astype(
+        jnp.bfloat16
+    )
     norms = jnp.einsum("rd,rd->r", embeddings, embeddings, preferred_element_type=jnp.float32)
     chosen_norms = jnp.einsum("rd,rd->r", chosen, chosen, preferred_element_type=jnp.float32)
     dots = times_transposed(embeddings, chosen, False)

time: 716 us -> 1360 us (1.90)
  blocking collectives: 87.7 us -> 701 us
  waiting for transfers between devices: 255 us -> 287 us
    psum x1, blocking collectives: 87.7 us -> 701 us  [per_device(): jax.lax.psum(jax.lax.psum(picked, axis_name='sub'), axis_name='bank')]
    psum x0 -> x1, waiting for transfers between devices: none -> 31 us  [per_device(): jax.lax.psum(picked, axis_name='sub')]
  transfers between devices with their start and end apart: 1 -> 2, of which waited for: 1 -> 2; matrix products, arithmetic and copies ran while one was open for 0% -> 0% of each run, Pallas kernels for 0% -> 0%
where the time goes in v1:
time: 1360 us
  blocking collectives  701 us (52%)
  waiting for transfers between devices  287 us (21%)
  other arithmetic  244 us (18%)
  matrix products  67.7 us (5%)
  local copies, waits for them, and re-layouts  37.9 us (3%)
  between operations  19.9 us (1%)
    psum x1, blocking collectives, per_device(): jax.lax.psum(jax.lax.psum(picked, axis_name='sub'), axis_name='bank')  701 us
    psum x1, waiting for transfers between devices, per_device(): gram = lax.psum(local_gram, ('bank', 'sub'))  256 us
    another operation x15, other arithmetic, per_device(): lower_root = jnp.linalg.cholesky(gram)  81.3 us
    another operation x7, other arithmetic, lower_inverse(): lax.linalg.triangular_solve(factor, identity, left_side=True, lower=True)  80.1 us
    another operation x7, other arithmetic, per_device(): second_inverse = lower_inverse(jnp.linalg.cholesky(second_block))  34.6 us
    another operation x6, other arithmetic, per_device(): first_inverse = lower_inverse(jnp.linalg.cholesky(block[:P_SIZE, :P_SIZE]))  34 us
    dot_general x6, matrix products, times_transposed(): lax.dot_general(left, right, (((1,), (1,)), ((), ())), precision=lax.Prec...  31.8 us
    psum x1, waiting for transfers between devices, per_device(): jax.lax.psum(picked, axis_name='sub')  31 us
  transfers between devices with their start and end apart: 2, of which 2 were waited for; matrix products, arithmetic and copies ran while one was open for 0% of the time, Pallas kernels for 0%

profile of v1, /device:TPU:2, one launch (start us, length us, event | category | flops | bytes accessed | tf_op | source)
XLA Modules:
  0.0 1357.8 jit_solution(14624836880842670373)
XLA Ops:
  8.6 6.3 gather_fusion
  15.0 1.6 convert_multiply_fusion.2
  16.7 4.1 fusion
  20.8 31.0 %all-reduce.6.cloned.1.call-done = f32[512,1024]{1,0:T(8,128)} async-done(((f32[512,1024]{1,0:T(8,128)}), f32[512,1024]{1,0:T(8,128)}) %all-reduce.6.cloned.1.call-update) | async-done | bytes 2097168 | tf_op jit(solution)/shard_map/psum | solution.py:39
  51.8 700.8 %all-reduce.9 = bf16[512,1024]{1,0:T(8,128)(2,1)S(1)} all-reduce(f32[512,1024]{1,0:T(8,128)} %all-reduce.6.cloned.1.call-done), channel_id=1, replica_groups=mesh['bank'=128,'sub'=2] {'bank'}, use_global_device_ids=true, to_apply=%region_1.2 | all-reduce | flops 524288 | bytes 3145728 | tf_op jit(solution)/shard_map/psum | solution.py:39
  753.9 11.7 cholesky.357
  765.7 9.8 custom-call.43
  776.0 11.7 cholesky.367
  789.8 3.9 while.6
  790.4 1.3 bitcast_dynamic-update-slice_fusion.7
  792.4 1.3 bitcast_dynamic-update-slice_fusion.7
  793.8 20.1 %custom-call.44 = f32[2,128,128]{1,2,0:T(8,128)S(1)} custom-call(f32[2,128,128]{2,1,0:T(8,128)S(1)} %get-tuple-element.27), custom_call_target="InvertDiagBlocksLowerTriangular" | custom-call | tf_op jit(solution)/shard_map/triangular_solve/custom-call.9 | solution.py:11
  816.6 11.7 cholesky.384
  828.4 9.8 custom-call.45
  838.7 11.7 cholesky.394
  853.1 3.9 while.7
  857.0 19.9 %custom-call.46 = f32[2,128,128]{1,2,0:T(8,128)S(1)} custom-call(f32[2,128,128]{2,1,0:T(8,128)S(1)} %get-tuple-element.28), custom_call_target="InvertDiagBlocksLowerTriangular" | custom-call | tf_op jit(solution)/shard_map/triangular_solve/custom-call.9 | solution.py:11
  877.8 5.7 subtract_divide_fusion
  883.5 3.0 fusion.3
  886.5 3.2 convolution_subtract_fusion
  889.8 3.0 fusion.30
  892.8 1.7 copy-done
  894.4 11.9 fusion.17
  908.4 256.2 %all-reduce.8.cloned.1.call-done = f32[512,512]{0,1:T(8,128)} async-done(((f32[512,512]{0,1:T(8,128)}), f32[512,512]{0,1:T(8,128)}) %all-reduce.8.cloned.1.call-update) | async-done | bytes 1048592 | tf_op jit(solution)/shard_map/psum | solution.py:67
  1164.6 2.5 copy.12
  1167.1 1.8 fusion.14
  1169.9 11.7 cholesky.167
  1182.8 9.8 custom-call.35
  1192.6 1.9 constant_dynamic-update-slice_fusion.5
  1195.8 11.7 cholesky.190
  1209.5 9.9 custom-call.36
  1220.4 1.5 convolution_subtract_fusion.6
  1221.8 11.7 cholesky.294
  1234.9 9.8 custom-call.47
  1245.5 1.4 convolution_subtract_fusion.11
  1246.9 11.9 cholesky.307
  1262.8 2.8 fusion.16
  1265.6 13.8 %while.5 = (s32[]{:T(128)}, f32[512,512]{1,0:T(8,128)}, s32[4,2]{0,1:T(2,128)S(1)}, f32[4,128,128]{2,1,0:T(8,128)}, s32[]{:T(128)}) while((s32[]{:T(128)}, f32[512,512]{1,0:T(8,128)}, s32[4,2]{0,1:T(2,128)S(1)}, f32[4,128,128]{2,1,0:T(8,128)}, s32[]{:T(128)}) %tuple.78), condition=%wide.while_cond.1, body=%wide.while_body.1.sunk | while | flops 2 | bytes 132705 | solution.py:11
  1266.2 2.8 bitcast_dynamic-update-slice_fusion.6
  1269.7 2.8 bitcast_dynamic-update-slice_fusion.6
  1273.2 2.8 bitcast_dynamic-update-slice_fusion.6
  1276.7 2.7 bitcast_dynamic-update-slice_fusion.6
  1279.4 40.1 %custom-call.37 = f32[4,128,128]{1,2,0:T(8,128)S(1)} custom-call(f32[4,128,128]{2,1,0:T(8,128)} %get-tuple-element.20), custom_call_target="InvertDiagBlocksLowerTriangular" | custom-call | tf_op jit(solution)/shard_map/triangular_solve | solution.py:11
  1320.8 1.4 convolution_subtract_fusion.2
  1322.6 1.4 convolution_subtract_fusion.1
  1324.5 1.7 convolution_subtract_fusion.4
  1326.6 21.6 %fusion.1 = f32[3072,512]{1,0:T(8,128)} fusion(f32[3072,256]{0,1:T(8,128)S(1)} %copy-done.1, f32[3072,256]{0,1:T(8,128)S(1)} %fusion.3, f32[128,512]{1,0:T(8,128)S(1)} %fusion.50, f32[128,512]{1,0:T(8,128)S(1)} %fusion.51, f32[128,512]{1,0:T(8,128)S(1)} %fusion.53, f32[128,512]{1,0:T(8,128)S(1)} %fusion.37), kind=kOutput, calls=%fused_computation.11 | convolution fusion | flops 9666035712 | bytes 13631488 | tf_op jit(solution)/shard_map/dot_general | solution.py:16
  1348.2 2.5 copy.14
  (100 shorter events, 31.6 us)
Async XLA Ops:
  7.2 44.7 %all-reduce.6.cloned.1.call-start = ((), (), s32[]{:S(2)}) async-start(), calls=%async_computation | async-start | bytes 4194304 | tf_op jit(solution)/shard_map/psum | solution.py:39
  16.6 1148.0 %all-reduce.8.cloned.1.call-start = ((), (), s32[]{:S(2)}) async-start(), calls=%async_computation.1 | async-start | bytes 2097152 | tf_op jit(solution)/shard_map/psum | solution.py:67
  814.7 0.7 copy-start.3
  877.8 5.7 copy-start.4
  892.8 1.7 copy-start
  1168.9 1.0 copy-start.2
  1319.5 7.1 copy-start.1
Sparse Core Ops, SparseCore 0:
  16.7 35.0 all-reduce.5
  906.5 258.0 all-reduce.7
